TPU v7x, 512 devices: a whole 4x4x16 slice. The times are simulated.
512 devices in a mesh: req: 128 (over z, x, core), tp: 4 (over y).
Axes of the slice: x: 4, y: 4, z: 16, core: 2. Of those that a mesh axis runs over, the one named last changes fastest.
Arguments:
- tokens: bfloat16 [65536, 1408], P('req', 'tp'), may hold values from -24 to 24
- ln1_gain: float32 [1408], replicated, may hold values from 0.1 to 1.9
- ln1_bias: float32 [1408], replicated, may hold values from -3 to 3
- qkv_weight: bfloat16 [3, 1408, 1408], P(None, None, 'tp'), may hold values from -6 to 6
- out_weight: bfloat16 [1408, 1408], P('tp'), may hold values from -0.15625 to 0.15625
- ln2_gain: float32 [1408], replicated, may hold values from 0.25 to 1.75
- ln2_bias: float32 [1408], replicated, may hold values from -3 to 3
- merger_weight: bfloat16 [5632, 3584], P('req', 'tp'), may hold values from -0.078125 to 0.078125
- group_segments: int32 [128, 128], P('req'), may hold values from 0 to 7, never falling along the last dimension, each value on 1 to 41 neighbouring positions
- owners: int32 [16384, 1], P('req'), may hold values from 0 to 127; in each aligned block of 128 rows (0 to 127, 128 to 255, ...) at most 2 rows name the same one
Outputs:
- received: bfloat16 [32768, 3584], P('req', 'tp')
Inputs may be any that keep to these rules, and one draw needn't show every extreme that they name: `group_segments`: never falling along a request's groups; every picture has 1 to 41 groups and one has exactly 41. `owners`: among the 128 groups of one request no owner appears more than 2 times; in every draw some request sends exactly 2 to some owner.
All inputs are finite; a program needn't handle non-finite values.
Results may differ from a plain program's by a relative error of at most 0.009.
Values may be sent and summed in bfloat16 or wider, within the bound.
No kernel may reach another device: no remote copies, remote signals or barrier semaphores. Data moves between devices by JAX's collectives and lax.ppermute only.
A program may use at most 128 MiB of HBM per device.

v0:
```python
import jax
import jax.numpy as jnp
from jax import lax
from jax.sharding import PartitionSpec as P

HEAD_DIM = 88
epsilon = 1e-06


def local(
    tokens,
    ln1_gain,
    ln1_bias,
    qkv_weight,
    out_weight,
    ln2_gain,
    ln2_bias,
    merger_weight,
    group_segments,
    owners,
):
    tp_count = lax.axis_size("tp")
    req_count = lax.axis_size("req")
    col_width = tokens.shape[1]
    full_width = col_width * tp_count
    tok_count = tokens.shape[0]
    group_count = tok_count // 4
    out_cols = merger_weight.shape[1]
    gathered = lax.all_gather(tokens, "tp", axis=1, tiled=True).astype(jnp.float32)
    input_mean = jnp.mean(gathered, axis=1, keepdims=True)
    centered = gathered - input_mean
    input_var = jnp.mean(centered * centered, axis=1, keepdims=True)
    normed = (centered * lax.rsqrt(input_var + epsilon) * ln1_gain + ln1_bias).astype(jnp.bfloat16)
    combined = jnp.einsum("td,cdh->cth", normed, qkv_weight, preferred_element_type=jnp.float32)
    combined = combined.astype(jnp.bfloat16).reshape(3, tok_count, -1, HEAD_DIM)
    queries, key_heads, value_heads = (combined[0], combined[1], combined[2])
    segment_ids = jnp.repeat(group_segments[0], 4)
    same_picture = segment_ids[:, None] == segment_ids[None, :]
    scores = jnp.einsum(
        "qhd,khd->hqk", queries, key_heads, preferred_element_type=jnp.float32
    ) * HEAD_DIM ** (-0.5)
    scores = jnp.where(same_picture[None], scores, -1e30)
    row_max = jnp.max(scores, axis=2, keepdims=True)
    exponent = jnp.exp(scores - row_max)
    weights = (exponent / jnp.sum(exponent, axis=2, keepdims=True)).astype(jnp.bfloat16)
    context = jnp.einsum("hqk,khd->qhd", weights, value_heads, preferred_element_type=jnp.float32)
    context = context.astype(jnp.bfloat16).reshape(tok_count, -1)
    partial_value = jnp.dot(context, out_weight, preferred_element_type=jnp.float32)
    attended = lax.psum_scatter(
        partial_value.astype(jnp.bfloat16), "tp", scatter_dimension=1, tiled=True
    ).astype(jnp.float32)
    hidden = tokens.astype(jnp.float32) + attended
    row_total = lax.psum(jnp.sum(hidden, axis=1), "tp")
    row_mean = (row_total / full_width)[:, None]
    shifted = hidden - row_mean
    row_spread = lax.psum(jnp.sum(shifted * shifted, axis=1), "tp")
    variance = (row_spread / full_width)[:, None]
    offset = lax.axis_index("tp") * col_width
    gain_part = lax.dynamic_slice_in_dim(ln2_gain, offset, col_width)
    bias_part = lax.dynamic_slice_in_dim(ln2_bias, offset, col_width)
    patches = (shifted * lax.rsqrt(variance + epsilon) * gain_part + bias_part).astype(jnp.bfloat16)
    grouped = patches.reshape(group_count, 4, col_width)
    full_groups = lax.all_gather(grouped, "tp", axis=2, tiled=True)
    merged = full_groups.reshape(group_count, 4 * full_width)
    projected = jnp.dot(
        merged,
        lax.all_gather(merger_weight, "req", axis=0, tiled=True),
        preferred_element_type=jnp.float32,
    )
    projected = projected.astype(jnp.bfloat16)
    capacity = max(2, 2 * group_count // req_count)
    slot_count = req_count * capacity
    target = owners[:, 0]
    owner_ids = jnp.arange(req_count, dtype=jnp.int32)
    owner_hits = (target[:, None] == owner_ids[None, :]).astype(jnp.int32)
    before = jnp.cumsum(owner_hits, axis=0) - owner_hits
    slot_rank = jnp.sum(before * owner_hits, axis=1)
    slot_index = target * capacity + slot_rank
    placing = (slot_index[None, :] == jnp.arange(slot_count, dtype=jnp.int32)[:, None]).astype(
        jnp.bfloat16
    )
    outgoing = jnp.dot(placing, projected, preferred_element_type=jnp.float32).astype(jnp.bfloat16)
    outgoing = outgoing.reshape(req_count, capacity, out_cols)
    arrived = lax.all_to_all(outgoing, "req", split_axis=0, concat_axis=0, tiled=True)
    return arrived.reshape(slot_count, out_cols)


def solution(mesh):
    in_specs = (
        P("req", "tp"),
        P(),
        P(),
        P(None, None, "tp"),
        P("tp", None),
        P(),
        P(),
        P("req", "tp"),
        P("req", None),
        P("req", None),
    )
    out_specs = P("req", "tp")
    return jax.shard_map(local, mesh=mesh, in_specs=in_specs, out_specs=out_specs, check_vma=False)
```

profile of v0, /device:TPU:33, one launch (start us, length us, event | category | flops | bytes accessed | tf_op | source)
XLA Modules:
  0.0 379.6 jit_solution(7323851090388105527)
XLA Ops:
  6.5 0.0 copy-start
  6.5 0.0 copy-start.5
  6.5 0.0 copy-start.6
  6.5 0.0 all-gather.5.cloned.1.call-start
  6.5 0.7 all-gather.5.cloned.1.call-update
  7.3 0.0 reduce-scatter.2.cloned.1.call-start
  7.3 0.9 broadcast_in_dim.14
  8.2 0.1 eq.51
  8.3 0.9 broadcast_compare_fusion
  9.3 37.2 %all-gather.5.cloned.1.call-done = bf16[512,1408]{0,1:T(8,128)(2,1)} async-done(((bf16[512,352]{0,1:T(8,128)(2,1)}), bf16[512,1408]{0,1:T(8,128)(2,1)}) %all-gather.5.cloned.1.call-update) | async-done | bytes 1441808 | tf_op jit(solution)/shard_map/all_gather | solution.py:29
  46.5 0.0 copy-start.1
  46.5 1.7 convert_reduce_fusion
  48.2 1.8 fusion.4
  50.1 0.0 copy-done
  50.1 0.0 copy-done.5
  50.1 0.0 copy-done.6
  50.1 0.0 copy-done.1
  50.1 2.0 fusion.18
  52.1 0.9 fusion.30
  53.0 4.8 %fusion.31 = (f32[4,512]{1,0:T(4,128)S(1)}, f32[4,512,512]{1,2,0:T(8,128)}) fusion(pred[512,512]{0,1:T(8,128)(4,1)} %broadcast_compare_fusion, bf16[512,4,88]{0,2,1:T(8,128)(2,1)} %bitcast.31, bf16[512,4,88]{0,2,1:T(8,128)(2,1)} %bitcast.30), kind=kOutput, calls=%fused_computation.48 | convolution fusion | flops 188744192 | bytes 5185536 | tf_op jit(solution)/shard_map/sub | solution.py:44
  57.8 0.0 copy-start.3
  57.8 2.8 fusion.21
  60.6 0.0 copy-start.2
  60.6 0.0 copy-done.3
  60.6 2.1 convolution_convert_fusion
  62.7 0.0 reduce-scatter.2.cloned.1.call-update
  62.7 0.0 copy-start.4
  62.7 0.0 all-gather.7.cloned.1.call-start
  62.8 0.8 dynamic_slice.6
  63.5 0.8 dynamic_slice.7
  64.3 30.7 %reduce-scatter.2.cloned.1.call-done = bf16[512,352]{0,1:T(8,128)(2,1)} async-done(((bf16[512,1408]{0,1:T(8,128)(2,1)}), bf16[512,352]{0,1:T(8,128)(2,1)}) %reduce-scatter.2.cloned.1.call-update) | async-done | bytes 360464 | tf_op jit(solution)/shard_map/reduce_scatter | solution.py:49
  95.0 0.0 copy-done.2
  95.0 1.1 fusion.23
  96.1 7.6 %psum.14 = f32[512]{0:T(512)S(1)} all-reduce(f32[512]{0:T(512)S(1)} %fusion.23), channel_id=1, replica_groups=mesh['req'=128,'tp'=4] {'tp'}, use_global_device_ids=true, to_apply=%region_8.9 | all-reduce | flops 512 | bytes 4096 | tf_op jit(solution)/shard_map/psum | solution.py:53
  103.7 1.1 multiply_reduce_fusion
  104.9 6.0 %psum.15 = f32[512]{0:T(512)S(1)} all-reduce(f32[512]{0:T(512)S(1)} %multiply_reduce_fusion), channel_id=1, replica_groups=mesh['req'=128,'tp'=4] {'tp'}, use_global_device_ids=true, to_apply=%region_10.11 | all-reduce | flops 512 | bytes 4096 | tf_op jit(solution)/shard_map/psum | solution.py:56
  110.9 1.9 add_convert_fusion
  112.8 1.2 copy.19
  114.0 0.9 reshape.86
  114.8 2.1 copy.20
  116.9 0.0 all-gather.7.cloned.1.call-update
  116.9 0.0 all-gather.9.cloned.1.call-start
  117.0 0.5 all-gather.9.cloned.1.call-update
  117.5 0.0 copy-done.4
  117.5 0.1 fusion.27
  117.6 0.2 reduce_window_sum.11
  117.8 0.2 select_reduce_fusion
  118.0 36.7 %all-gather.7.cloned.1.call-done = bf16[128,4,1408]{0,1,2:T(4,128)(2,1)} async-done(((bf16[128,4,352]{0,1,2:T(4,128)(2,1)}), bf16[128,4,1408]{0,1,2:T(4,128)(2,1)}) %all-gather.7.cloned.1.call-update) | async-done | bytes 1441808 | tf_op jit(solution)/shard_map/all_gather | solution.py:63
  154.7 2.7 copy.21
  157.4 151.2 %all-gather.9.cloned.1.call-done = bf16[128,44,896]{2,1,0:T(8,128)(2,1)} async-done(((bf16[1,44,896]{2,1,0:T(8,128)(2,1)}), bf16[128,44,896]{2,1,0:T(8,128)(2,1)}) %all-gather.9.cloned.1.call-update) | async-done | bytes 10092560 | tf_op jit(solution)/shard_map/all_gather | solution.py:67
  308.6 13.4 %reshape.91 = bf16[5632,896]{1,0:T(8,128)(2,1)} reshape(bf16[128,44,896]{2,1,0:T(8,128)(2,1)} %all-gather.9.cloned.1.call-done) | data formatting | bytes 20185088
  322.0 7.0 %convolution_convert_fusion.2 = bf16[256,896]{1,0:T(8,128)(2,1)} fusion(bf16[128,5632]{0,1:T(8,128)(2,1)} %bitcast.28, bf16[5632,896]{1,0:T(8,128)(2,1)} %reshape.91, s32[128]{0:T(128)S(1)} %multiply_add_fusion), kind=kOutput, calls=%fused_computation.25 | convolution fusion | flops 1350942720 | bytes 11993600 | tf_op jit(solution)/shard_map/dot_general | solution.py:82
  329.0 1.2 reshape.88
  330.2 40.9 %all_to_all.5 = bf16[128,2,896]{2,1,0:T(2,128)(2,1)} all-to-all(bf16[128,2,896]{2,1,0:T(2,128)(2,1)S(1)} %reshape.88), channel_id=1, replica_groups=mesh['req'=128,'tp'=4] {'req'}, dimensions={0} | all-to-all | bytes 917504 | tf_op jit(solution)/shard_map/all_to_all | solution.py:84
  371.1 2.0 reshape.89
  (5 shorter events, 0.0 us)
Async XLA Ops:
  6.5 43.5 %copy-start = (bf16[3,1408,352]{1,2,0:T(8,128)(2,1)S(1)}, bf16[3,1408,352]{1,2,0:T(8,128)(2,1)}, u32[]{:S(2)}) copy-start(bf16[3,1408,352]{1,2,0:T(8,128)(2,1)} %param.13) | copy-start | bytes 8921092
  6.5 43.5 %copy-start.5 = (f32[1408]{0:T(1024)S(1)}, f32[1408]{0:T(1024)}, u32[]{:S(2)}) copy-start(f32[1408]{0:T(1024)} %param.12) | copy-start | bytes 16900
  6.5 43.5 %copy-start.6 = (f32[1408]{0:T(1024)S(1)}, f32[1408]{0:T(1024)}, u32[]{:S(2)}) copy-start(f32[1408]{0:T(1024)} %param.11) | copy-start | bytes 16900
  6.5 40.0 %all-gather.5.cloned.1.call-start = ((), (), s32[]{:S(2)}) async-start(), calls=%async_computation.2 | async-start | bytes 1802240 | tf_op jit(solution)/shard_map/all_gather | solution.py:29
  7.3 87.8 %reduce-scatter.2.cloned.1.call-start = ((), (), s32[]{:S(2)}) async-start(), calls=%async_computation.3 | async-start | bytes 1802240 | tf_op jit(solution)/shard_map/reduce_scatter | solution.py:49
  46.5 3.6 copy-start.1
  57.8 2.8 copy-start.3
  60.6 34.5 %copy-start.2 = (bf16[512,352]{0,1:T(8,128)(2,1)S(1)}, bf16[512,352]{0,1:T(8,128)(2,1)}, u32[]{:S(2)}) copy-start(bf16[512,352]{0,1:T(8,128)(2,1)} %param.10) | copy-start | bytes 1081348
  62.7 54.8 %copy-start.4 = (s32[128,1]{0,1:T(1,128)S(1)}, s32[128,1]{0,1:T(1,128)}, u32[]{:S(2)}) copy-start(s32[128,1]{0,1:T(1,128)} %param.19) | copy-start | bytes 1540
  62.7 92.0 %all-gather.7.cloned.1.call-start = ((), (), s32[]{:S(2)}) async-start(), calls=%async_computation.4 | async-start | bytes 1802240 | tf_op jit(solution)/shard_map/all_gather | solution.py:63
  116.9 191.6 %all-gather.9.cloned.1.call-start = ((), (), s32[]{:S(2)}) async-start(), calls=%async_computation.5 | async-start | bytes 11096064 | tf_op jit(solution)/shard_map/all_gather | solution.py:67
Sparse Core Ops, SparseCore 0:
  9.4 37.0 all-gather.4
  62.8 32.1 reduce-scatter.1
  117.1 37.5 all-gather.6
  157.6 150.9 all-gather.8
where the time goes:
time: 381 us; the launch traced here: 380 us
  waiting for transfers between devices  257 us (67%)
  blocking collectives  54.5 us (14%)
  local copies, waits for them, and re-layouts  26.9 us (7%)
  matrix products  18.7 us (5%)
  between operations  13.3 us (3%)
  other arithmetic  9.11 us (2%)
    all_gather x1, waiting for transfers between devices, local(): lax.all_gather(merger_weight, 'req', axis=0, tiled=True)  151 us
    all_to_all x1, blocking collectives, local(): lax.all_to_all(outgoing, 'req', split_axis=0, concat_axis=0, tiled=True)  40.9 us
    all_gather x1, waiting for transfers between devices, local(): lax.all_gather(tokens, 'tp', axis=1, tiled=True).astype(jnp.float32)  37.2 us
    all_gather x1, waiting for transfers between devices, local(): full_groups = lax.all_gather(grouped, 'tp', axis=2, tiled=True)  36.7 us
    reduce_scatter x1, waiting for transfers between devices, local(): lax.psum_scatter(partial_value.astype(jnp.bfloat16), 'tp', scatter_dimens...  30.7 us
    unnamed x15, local copies, waits for them, and re-layouts  13.4 us
  transfers between devices with their start and end apart: 4, of which 4 were waited for; matrix products, arithmetic and copies ran while one was open for 2% of the time, Pallas kernels for 0%

commit v1 on v0

--- a/solution.py
+++ b/solution.py
@@ -60,7 +60,9 @@
     bias_part = lax.dynamic_slice_in_dim(ln2_bias, offset, col_width)
     patches = (shifted * lax.rsqrt(variance + epsilon) * gain_part + bias_part).astype(jnp.bfloat16)
     grouped = patches.reshape(group_count, 4, col_width)
-    full_groups = lax.all_gather(grouped, "tp", axis=2, tiled=True)
+    full_groups = jnp.concatenate(
+        lax.all_to_all(jnp.stack([grouped] * lax.axis_size("tp")), "tp", 0, 0), axis=2
+    )
     merged = full_groups.reshape(group_count, 4 * full_width)
     projected = jnp.dot(
         merged,

time: 381 us -> 291 us (0.76)
  waiting for transfers between devices: 257 us -> 160 us
  starting transfers between devices: 0.12 us -> 4.42 us
    all_gather x1, waiting for transfers between devices: 151 us -> 78.2 us  [local(): lax.all_gather(merger_weight, 'req', axis=0, tiled=True)]
    all_gather x1 -> x0, waiting for transfers between devices: 36.7 us -> none  [local(): full_groups = lax.all_gather(grouped, 'tp', axis=2, tiled=True)]
    all_to_all x0 -> x1, waiting for transfers between devices: none -> 13.6 us  [local(): lax.all_to_all(jnp.stack([grouped] * lax.axis_size('tp')), 'tp', 0, 0)]
    all_to_all x0 -> x1, starting transfers between devices: none -> 4.33 us  [local(): lax.all_to_all(jnp.stack([grouped] * lax.axis_size('tp')), 'tp', 0, 0)]
  transfers between devices with their start and end apart: 4 -> 4, of which waited for: 4 -> 4; matrix products, arithmetic and copies ran while one was open for 2% -> 5% of each run, Pallas kernels for 0% -> 0%
where the time goes in v1:
time: 291 us; the launch traced here: 290 us
  waiting for transfers between devices  160 us (55%)
  blocking collectives  55.1 us (19%)
  local copies, waits for them, and re-layouts  27.3 us (9%)
  matrix products  18.6 us (6%)
  between operations  15 us (5%)
  other arithmetic  9.11 us (3%)
  starting transfers between devices  4.42 us (2%)
    all_gather x1, waiting for transfers between devices, local(): lax.all_gather(merger_weight, 'req', axis=0, tiled=True)  78.2 us
    all_to_all x1, blocking collectives, local(): lax.all_to_all(outgoing, 'req', split_axis=0, concat_axis=0, tiled=True)  41 us
    all_gather x1, waiting for transfers between devices, local(): lax.all_gather(tokens, 'tp', axis=1, tiled=True).astype(jnp.float32)  37.2 us
    reduce_scatter x1, waiting for transfers between devices, local(): lax.psum_scatter(partial_value.astype(jnp.bfloat16), 'tp', scatter_dimens...  30.2 us
    all_to_all x1, waiting for transfers between devices, local(): lax.all_to_all(jnp.stack([grouped] * lax.axis_size('tp')), 'tp', 0, 0)  13.6 us
    unnamed x15, local copies, waits for them, and re-layouts  13.4 us
    psum x1, blocking collectives, local(): row_total = lax.psum(jnp.sum(hidden, axis=1), 'tp')  7.81 us
    dot_general x1, matrix products, local(): jnp.dot(placing, projected, preferred_element_type=jnp.float32)  7.03 us
  transfers between devices with their start and end apart: 4, of which 4 were waited for; matrix products, arithmetic and copies ran while one was open for 5% of the time, Pallas kernels for 0%

profile of v1, /device:TPU:33, one launch (start us, length us, event | category | flops | bytes accessed | tf_op | source)
XLA Modules:
  0.0 290.0 jit_solution(3039078731299941668)
XLA Ops:
  7.4 0.0 copy-start
  7.4 0.0 copy-start.5
  7.4 0.0 copy-start.6
  7.4 0.0 all-gather.4.cloned.1.call-start
  7.4 0.7 all-gather.4.cloned.1.call-update
  8.1 0.0 reduce-scatter.2.cloned.1.call-start
  8.1 0.9 broadcast_in_dim.14
  9.0 0.1 eq.51
  9.1 0.9 broadcast_compare_fusion
  10.1 37.2 %all-gather.4.cloned.1.call-done = bf16[512,1408]{0,1:T(8,128)(2,1)} async-done(((bf16[512,352]{0,1:T(8,128)(2,1)}), bf16[512,1408]{0,1:T(8,128)(2,1)}) %all-gather.4.cloned.1.call-update) | async-done | bytes 1441808 | tf_op jit(solution)/shard_map/all_gather | solution.py:29
  47.3 0.0 copy-start.1
  47.3 1.7 convert_reduce_fusion
  49.1 1.8 fusion.4
  50.9 0.0 copy-done
  50.9 0.0 copy-done.5
  50.9 0.0 copy-done.6
  50.9 0.0 copy-done.1
  50.9 2.0 fusion.18
  52.9 0.9 fusion.30
  53.8 4.8 %fusion.31 = (f32[4,512]{1,0:T(4,128)S(1)}, f32[4,512,512]{1,2,0:T(8,128)}) fusion(pred[512,512]{0,1:T(8,128)(4,1)} %broadcast_compare_fusion, bf16[512,4,88]{0,2,1:T(8,128)(2,1)} %bitcast.33, bf16[512,4,88]{0,2,1:T(8,128)(2,1)} %bitcast.32), kind=kOutput, calls=%fused_computation.48 | convolution fusion | flops 188744192 | bytes 5185536 | tf_op jit(solution)/shard_map/sub | solution.py:44
  58.6 0.0 copy-start.3
  58.6 2.8 fusion.21
  61.4 0.0 copy-start.2
  61.4 0.0 copy-done.3
  61.4 2.1 convolution_convert_fusion
  63.5 0.0 reduce-scatter.2.cloned.1.call-update
  63.5 0.0 all-gather.6.cloned.1.call-start
  63.6 0.5 all-gather.6.cloned.1.call-update
  64.1 0.8 dynamic_slice.6
  64.9 0.8 dynamic_slice.7
  65.6 30.2 %reduce-scatter.2.cloned.1.call-done = bf16[512,352]{0,1:T(8,128)(2,1)} async-done(((bf16[512,1408]{0,1:T(8,128)(2,1)}), bf16[512,352]{0,1:T(8,128)(2,1)}) %reduce-scatter.2.cloned.1.call-update) | async-done | bytes 360464 | tf_op jit(solution)/shard_map/reduce_scatter | solution.py:49
  95.8 0.0 copy-done.2
  95.9 1.1 fusion.23
  97.0 7.8 %psum.14 = f32[512]{0:T(512)S(1)} all-reduce(f32[512]{0:T(512)S(1)} %fusion.23), channel_id=1, replica_groups=mesh['req'=128,'tp'=4] {'tp'}, use_global_device_ids=true, to_apply=%region_8.9 | all-reduce | flops 512 | bytes 4096 | tf_op jit(solution)/shard_map/psum | solution.py:53
  104.8 1.1 multiply_reduce_fusion
  105.9 6.3 %psum.15 = f32[512]{0:T(512)S(1)} all-reduce(f32[512]{0:T(512)S(1)} %multiply_reduce_fusion), channel_id=1, replica_groups=mesh['req'=128,'tp'=4] {'tp'}, use_global_device_ids=true, to_apply=%region_10.11 | all-reduce | flops 512 | bytes 4096 | tf_op jit(solution)/shard_map/psum | solution.py:56
  112.2 1.9 add_convert_fusion
  114.2 1.2 copy.20
  115.4 0.9 stack_reshape.2
  116.2 0.0 copy-start.4
  116.2 1.3 copy.21
  117.5 1.4 stack.3
  118.9 4.3 %all-to-all-start = ((bf16[4,128,4,352]{1,3,2,0:T(8,128)(2,1)}), bf16[4,128,4,352]{1,3,2,0:T(8,128)(2,1)}, u32[]{:S(2)}, u32[]{:S(2)}) async-start(bf16[4,128,4,352]{1,3,2,0:T(8,128)(2,1)} %stack.3), calls=%async_computation.1 | async-start | bytes 2883584 | tf_op jit(solution)/shard_map/all_to_all | solution.py:64
  123.2 0.0 copy-done.4
  123.2 0.1 fusion.27
  123.3 0.2 reduce_window_sum.11
  123.5 0.2 select_reduce_fusion
  123.7 13.6 %all-to-all-done = bf16[4,128,4,352]{1,3,2,0:T(8,128)(2,1)} async-done(((bf16[4,128,4,352]{1,3,2,0:T(8,128)(2,1)}), bf16[4,128,4,352]{1,3,2,0:T(8,128)(2,1)}, u32[]{:S(2)}, u32[]{:S(2)}) %all-to-all-start) | async-done | bytes 1441824 | tf_op jit(solution)/shard_map/all_to_all | solution.py:64
  137.2 2.6 copy.22
  139.8 78.2 %all-gather.6.cloned.1.call-done = bf16[128,44,896]{2,1,0:T(8,128)(2,1)} async-done(((bf16[1,44,896]{2,1,0:T(8,128)(2,1)}), bf16[128,44,896]{2,1,0:T(8,128)(2,1)}) %all-gather.6.cloned.1.call-update) | async-done | bytes 10092560 | tf_op jit(solution)/shard_map/all_gather | solution.py:69
  218.0 13.4 %reshape.89 = bf16[5632,896]{1,0:T(8,128)(2,1)} reshape(bf16[128,44,896]{2,1,0:T(8,128)(2,1)} %all-gather.6.cloned.1.call-done) | data formatting | bytes 20185088
  231.4 7.0 %convolution_convert_fusion.2 = bf16[256,896]{1,0:T(8,128)(2,1)} fusion(bf16[128,5632]{0,1:T(8,128)(2,1)} %bitcast.30, bf16[5632,896]{1,0:T(8,128)(2,1)} %reshape.89, s32[128]{0:T(128)S(1)} %multiply_add_fusion), kind=kOutput, calls=%fused_computation.25 | convolution fusion | flops 1350942720 | bytes 11993600 | tf_op jit(solution)/shard_map/dot_general | solution.py:84
  238.5 1.2 reshape.86
  239.6 41.0 %all_to_all.10 = bf16[128,2,896]{2,1,0:T(2,128)(2,1)} all-to-all(bf16[128,2,896]{2,1,0:T(2,128)(2,1)S(1)} %reshape.86), channel_id=1, replica_groups=mesh['req'=128,'tp'=4] {'req'}, dimensions={0} | all-to-all | bytes 917504 | tf_op jit(solution)/shard_map/all_to_all | solution.py:86
  280.6 2.0 reshape.87
  (5 shorter events, 0.0 us)
Async XLA Ops:
  7.4 43.5 %copy-start = (bf16[3,1408,352]{1,2,0:T(8,128)(2,1)S(1)}, bf16[3,1408,352]{1,2,0:T(8,128)(2,1)}, u32[]{:S(2)}) copy-start(bf16[3,1408,352]{1,2,0:T(8,128)(2,1)} %param.13) | copy-start | bytes 8921092
  7.4 43.5 %copy-start.5 = (f32[1408]{0:T(1024)S(1)}, f32[1408]{0:T(1024)}, u32[]{:S(2)}) copy-start(f32[1408]{0:T(1024)} %param.12) | copy-start | bytes 16900
  7.4 43.5 %copy-start.6 = (f32[1408]{0:T(1024)S(1)}, f32[1408]{0:T(1024)}, u32[]{:S(2)}) copy-start(f32[1408]{0:T(1024)} %param.11) | copy-start | bytes 16900
  7.4 40.0 %all-gather.4.cloned.1.call-start = ((), (), s32[]{:S(2)}) async-start(), calls=%async_computation.3 | async-start | bytes 1802240 | tf_op jit(solution)/shard_map/all_gather | solution.py:29
  8.1 87.8 %reduce-scatter.2.cloned.1.call-start = ((), (), s32[]{:S(2)}) async-start(), calls=%async_computation.4 | async-start | bytes 1802240 | tf_op jit(solution)/shard_map/reduce_scatter | solution.py:49
  47.3 3.6 %copy-start.1 = (bf16[512,1408]{0,1:T(8,128)(2,1)S(1)}, bf16[512,1408]{0,1:T(8,128)(2,1)}, u32[]{:S(2)}) copy-start(bf16[512,1408]{0,1:T(8,128)(2,1)} %all-gather.4.cloned.1.call-done) | copy-start | bytes 4325380
  58.6 2.8 copy-start.3
  61.4 34.4 %copy-start.2 = (bf16[512,352]{0,1:T(8,128)(2,1)S(1)}, bf16[512,352]{0,1:T(8,128)(2,1)}, u32[]{:S(2)}) copy-start(bf16[512,352]{0,1:T(8,128)(2,1)} %param.10) | copy-start | bytes 1081348
  63.5 154.5 %all-gather.6.cloned.1.call-start = ((), (), s32[]{:S(2)}) async-start(), calls=%async_computation.5 | async-start | bytes 11096064 | tf_op jit(solution)/shard_map/all_gather | solution.py:69
  116.2 7.0 %copy-start.4 = (s32[128,1]{0,1:T(1,128)S(1)}, s32[128,1]{0,1:T(1,128)}, u32[]{:S(2)}) copy-start(s32[128,1]{0,1:T(1,128)} %param.19) | copy-start | bytes 1540
  118.9 18.4 %all-to-all-start = ((bf16[4,128,4,352]{1,3,2,0:T(8,128)(2,1)}), bf16[4,128,4,352]{1,3,2,0:T(8,128)(2,1)}, u32[]{:S(2)}, u32[]{:S(2)}) async-start(bf16[4,128,4,352]{1,3,2,0:T(8,128)(2,1)} %stack.3), calls=%async_computation.1 | async-start | bytes 2883584 | tf_op jit(solution)/shard_map/all_to_all | solution.py:64
Sparse Core Ops, SparseCore 0:
  10.3 37.0 all-gather.3
  63.6 32.1 reduce-scatter.1
Sparse Core Ops, SparseCore 1:
  67.0 150.9 all-gather.5
